TPU v7x, 512 devices: a whole 4x4x16 slice. The times are simulated.
512 devices in a mesh: img: 64 (over y, z), lm: 8 (over x, core).
Axes of the slice: x: 4, y: 4, z: 16, core: 2. Of those that a mesh axis runs over, the one named last changes fastest.
Arguments:
- jac_point: float32 [6, 1048576], P(None, ('img', 'lm')), may hold values from -4 to 4
- jac_cam: bfloat16 [1048576, 256], P(('img', 'lm')), may hold values from -0.125 to 0.125
- resid: float32 [2, 1048576], P(None, ('img', 'lm')), may hold values from -6 to 6
- point_ids: int32 [1048576], P(('img', 'lm')), may hold values from 0 to 4095
- cam_ids: int32 [1048576], P(('img', 'lm')), may hold values from 0 to 1023
- owner_slot: int32 [1024], replicated, may hold values from 0 to 1023, each once
- damping: float32 [1], replicated, may hold values from 0.1 to 1
Outputs:
- landmark_step: float32 [3, 32768], P(None, 'lm')
- camera_gradient: float32 [1024, 128], P(('img', 'lm'))
All inputs are finite; a program needn't handle non-finite values.
Results may differ from a plain program's by a relative error of at most 0.0029.
Values sent between devices are 32-bit elements; how exact they have to be, the bound alone decides.
No kernel may reach another device: no remote copies, remote signals or barrier semaphores. Data moves between devices by JAX's collectives and lax.ppermute only.
A program may use at most 64 MiB of HBM per device.

v0:
```python
import jax
import jax.numpy as jnp
from jax import lax
from jax.sharding import PartitionSpec as P

CAMP = 128
BLOCK = 64
LM_BLOCKS = 64


def obs_terms(jac_point, resid):
    u0, u1, u2 = (jac_point[0], jac_point[1], jac_point[2])
    v0, v1, v2 = (jac_point[3], jac_point[4], jac_point[5])
    ru, rv = (resid[0], resid[1])
    return jnp.stack(
        [
            u0 * u0 + v0 * v0,
            u0 * u1 + v0 * v1,
            u0 * u2 + v0 * v2,
            u1 * u1 + v1 * v1,
            u1 * u2 + v1 * v2,
            u2 * u2 + v2 * v2,
            u0 * ru + v0 * rv,
            u1 * ru + v1 * rv,
            u2 * ru + v2 * rv,
        ],
        axis=1,
    )


def solve_points(stats, damping):
    factor = damping[0]
    h01, h02, h12 = (stats[1], stats[2], stats[4])
    a00 = stats[0] + factor * (stats[0] + 1.0)
    a11 = stats[3] + factor * (stats[3] + 1.0)
    a22 = stats[5] + factor * (stats[5] + 1.0)
    g0, g1, g2 = (stats[6], stats[7], stats[8])
    c00 = a11 * a22 - h12 * h12
    c01 = h02 * h12 - h01 * a22
    c02 = h01 * h12 - h02 * a11
    c11 = a00 * a22 - h02 * h02
    c12 = h01 * h02 - a00 * h12
    c22 = a00 * a11 - h01 * h01
    determ = a00 * c00 + h01 * c01 + h02 * c02
    s0 = -(c00 * g0 + c01 * g1 + c02 * g2) / determ
    s1 = -(c01 * g0 + c11 * g1 + c12 * g2) / determ
    s2 = -(c02 * g0 + c12 * g1 + c22 * g2) / determ
    return jnp.stack([s0, s1, s2], axis=0)


def per_device(jac_point, jac_cam, resid, point_ids, cam_ids, owner_slot, damping):
    slice_points = LM_BLOCKS * BLOCK
    terms = obs_terms(jac_point, resid)
    local_stats = jax.ops.segment_sum(terms, point_ids, num_segments=slice_points).T
    stats = lax.psum(local_stats, "img")
    step = solve_points(stats, damping)
    step_obs = jnp.take(step, point_ids, axis=1)
    cu = (
        resid[0]
        + jac_point[0] * step_obs[0]
        + jac_point[1] * step_obs[1]
        + jac_point[2] * step_obs[2]
    )
    cv = (
        resid[1]
        + jac_point[3] * step_obs[0]
        + jac_point[4] * step_obs[1]
        + jac_point[5] * step_obs[2]
    )
    cu_half = cu.astype(jnp.bfloat16)
    cv_half = cv.astype(jnp.bfloat16)
    slots = jnp.take(owner_slot, cam_ids)
    groups_all = owner_slot.shape[0]
    n_obs = cam_ids.shape[0]
    width = min(1024, n_obs)
    group_iota = jnp.arange(groups_all, dtype=jnp.int32)[:, None]
    partial_grad = jnp.zeros((groups_all, CAMP), jnp.float32)
    for block_index in range(n_obs // width):
        lo_row = block_index * width
        block_slots = slots[lo_row : lo_row + width]
        member = (block_slots[None, :] == group_iota).astype(jnp.bfloat16)
        left_u = member * cu_half[None, lo_row : lo_row + width]
        left_v = member * cv_half[None, lo_row : lo_row + width]
        cam_block = jac_cam[lo_row : lo_row + width]
        partial_grad = partial_grad + jnp.dot(
            left_u, cam_block[:, :CAMP], preferred_element_type=jnp.float32
        )
        partial_grad = partial_grad + jnp.dot(
            left_v, cam_block[:, CAMP:], preferred_element_type=jnp.float32
        )
    gradient = lax.psum_scatter(partial_grad, ("img", "lm"), scatter_dimension=0, tiled=True)
    return (step, gradient)


def solution(mesh):
    placed = (
        P(None, ("img", "lm")),
        P(("img", "lm"), None),
        P(None, ("img", "lm")),
        P(("img", "lm")),
        P(("img", "lm")),
        P(),
        P(),
    )
    return jax.shard_map(
        per_device,
        mesh=mesh,
        in_specs=placed,
        out_specs=(P(None, "lm"), P(("img", "lm"), None)),
        check_vma=False,
    )
```

profile of v0, /device:TPU:4, one launch (start us, length us, event | category | flops | bytes accessed | tf_op | source)
XLA Modules:
  0.0 778.8 jit_solution(16912296263779753748)
XLA Ops:
  7.2 0.0 copy-start
  7.2 0.0 all-reduce.4.cloned.1.call-start
  7.2 1.1 add_bitcast_fusion.5
  8.4 1.2 add_bitcast_fusion
  9.5 0.1 stack.4
  9.7 0.4 copy.119
  10.0 0.0 copy-start.5
  10.0 0.0 copy-start.4
  10.0 12.1 %scatter_custom_fusion = f32[4096,9]{1,0:T(8,128)S(1)} fusion(s32[2048]{0:T(1024)} %param.10, f32[2048,9]{1,0:T(8,128)S(1)} %copy.119, f32[]{:T(128)} %constant.30.clone.1), kind=kCustom, calls=%fused_computation.28 | custom fusion | flops 18432 | bytes 147968 | tf_op jit(solution)/shard_map/scatter-add | solution.py:54
  22.1 1.3 copy.120
  23.5 0.0 all-reduce.4.cloned.1.call-update
  23.5 0.0 all-reduce.6.cloned.1.call-start
  23.5 0.0 copy-done.5
  24.2 0.0 copy-done.4
  24.2 0.0 copy-done
  24.2 8.6 %gather_fusion = s32[2048]{0:T(1024)S(1)} fusion(s32[1024]{0:T(1024)S(1)} %copy-done, s32[2048]{0:T(1024)S(1)} %fusion.39), kind=kCustom, calls=%fused_computation | custom fusion | bytes 24576 | tf_op jit(solution)/shard_map/jit(_take)/gather | solution.py:72
  32.8 0.0 copy-start.1
  32.9 0.0 copy-start.3
  32.9 261.6 %all-reduce.4.cloned.1.call-done = f32[9,4096]{1,0:T(8,128)} async-done(((f32[9,4096]{1,0:T(8,128)}), f32[9,4096]{1,0:T(8,128)}) %all-reduce.4.cloned.1.call-update) | async-done | bytes 147472 | tf_op jit(solution)/shard_map/psum | solution.py:55
  294.5 1.7 negate_divide_fusion.2
  296.3 1.8 negate_divide_fusion.1
  298.1 0.0 copy-start.2
  298.1 0.6 copy.121
  298.8 5.5 gather_fusion.1
  304.2 0.3 copy.122
  304.6 0.0 copy-done.1
  304.6 0.0 copy-done.3
  304.6 0.1 add_convert_fusion
  304.7 0.1 slice_reduce_fusion
  304.7 0.0 copy-start.6
  304.8 1.7 fusion.4
  306.5 0.0 copy-done.2
  306.5 0.0 copy-done.6
  306.5 0.7 fusion.22
  307.2 0.7 fusion.19
  308.0 1.5 fusion.16
  309.5 0.0 all-reduce.6.cloned.1.call-update
  309.5 461.2 %all-reduce.6.cloned.1.call-done = f32[1024,128]{1,0:T(8,128)} async-done(((f32[1024,128]{1,0:T(8,128)}), f32[1024,128]{1,0:T(8,128)}) %all-reduce.6.cloned.1.call-update) | async-done | bytes 524304
  770.7 1.2 constant_dynamic-slice_fusion
  (7 shorter events, 0.1 us)
Async XLA Ops:
  7.2 17.1 %copy-start = (s32[1024]{0:T(1024)S(1)}, s32[1024]{0:T(1024)}, u32[]{:S(2)}) copy-start(s32[1024]{0:T(1024)} %param.12) | copy-start | bytes 12292
  7.2 287.4 %all-reduce.4.cloned.1.call-start = ((), (), s32[]{:S(2)}) async-start(), calls=%async_computation | async-start | bytes 524288 | tf_op jit(solution)/shard_map/psum | solution.py:55
  10.0 13.5 %copy-start.5 = (s32[2048]{0:T(1024)S(1)}, s32[2048]{0:T(1024)}, u32[]{:S(2)}) copy-start(s32[2048]{0:T(1024)} %param.10) | copy-start | bytes 24580
  10.0 14.2 %copy-start.4 = (s32[2048]{0:T(1024)S(1)}, s32[2048]{0:T(1024)}, u32[]{:S(2)}) copy-start(s32[2048]{0:T(1024)} %param.11) | copy-start | bytes 24580
  23.5 747.2 %all-reduce.6.cloned.1.call-start = ((), (), s32[]{:S(2)}) async-start(), calls=%async_computation.1 | async-start | bytes 1048576
  32.8 271.8 %copy-start.1 = (f32[6,2048]{1,0:T(8,128)S(1)}, f32[6,2048]{1,0:T(8,128)}, u32[]{:S(2)}) copy-start(f32[6,2048]{1,0:T(8,128)} %param.7) | copy-start | bytes 147460
  32.9 271.8 %copy-start.3 = (f32[2,2048]{1,0:T(2,128)S(1)}, f32[2,2048]{1,0:T(2,128)}, u32[]{:S(2)}) copy-start(f32[2,2048]{1,0:T(2,128)} %param.9) | copy-start | bytes 49156
  298.1 8.4 %copy-start.2 = (f32[3,4096]{1,0:T(4,128)}, f32[3,4096]{1,0:T(4,128)S(1)}, u32[]{:S(2)}) copy-start(f32[3,4096]{1,0:T(4,128)S(1)} %pad_maximum_fusion) | copy-start | bytes 147460
  304.7 1.8 copy-start.6
Sparse Core Ops, SparseCore 0:
  23.6 270.8 all-reduce.3
  309.6 461.0 all-reduce.5
where the time goes:
time: 779 us
  waiting for transfers between devices  723 us (93%)
  local copies, waits for them, and re-layouts  18.2 us (2%)
  other arithmetic  18.1 us (2%)
  between operations  14.9 us (2%)
    unnamed x3, waiting for transfers between devices  461 us
    psum x1, waiting for transfers between devices, per_device(): stats = lax.psum(local_stats, 'img')  262 us
  transfers between devices with their start and end apart: 2, of which 2 were waited for; matrix products, arithmetic and copies ran while one was open for 1% of the time, Pallas kernels for 0%

commit v1 on v0

--- a/solution.py
+++ b/solution.py
@@ -52,7 +52,7 @@
     slice_points = LM_BLOCKS * BLOCK
     terms = obs_terms(jac_point, resid)
     local_stats = jax.ops.segment_sum(terms, point_ids, num_segments=slice_points).T
-    stats = lax.psum(local_stats, "img")
+    stats = jnp.sum(lax.all_gather(local_stats, "img"), axis=0)
     step = solve_points(stats, damping)
     step_obs = jnp.take(step, point_ids, axis=1)
     cu = (

time: 779 us -> 711 us (0.913)
  waiting for transfers between devices: 723 us -> 651 us
    psum x1 -> x0, waiting for transfers between devices: 262 us -> none  [per_device(): stats = lax.psum(local_stats, 'img')]
    all_gather x0 -> x1, waiting for transfers between devices: none -> 188 us  [per_device(): stats = jnp.sum(lax.all_gather(local_stats, 'img'), axis=0)]
where the time goes in v1:
time: 711 us
  waiting for transfers between devices  651 us (92%)
  other arithmetic  21.9 us (3%)
  local copies, waits for them, and re-layouts  18.2 us (3%)
  between operations  14.9 us (2%)
    unnamed x3, waiting for transfers between devices  463 us
    all_gather x1, waiting for transfers between devices, per_device(): stats = jnp.sum(lax.all_gather(local_stats, 'img'), axis=0)  188 us
  transfers between devices with their start and end apart: 2, of which 2 were waited for; matrix products, arithmetic and copies ran while one was open for 1% of the time, Pallas kernels for 0%

profile of v1, /device:TPU:4, one launch (start us, length us, event | category | flops | bytes accessed | tf_op | source)
XLA Modules:
  0.0 710.7 jit_solution(2357913751743429483)
XLA Ops:
  7.2 0.0 copy-start
  7.2 0.0 all-gather.4.cloned.1.call-start
  7.2 1.1 add_bitcast_fusion.5
  8.4 1.2 add_bitcast_fusion
  9.6 0.1 stack.4
  9.7 0.4 copy.95
  10.1 0.0 copy-start.4
  10.1 12.1 %scatter_custom_fusion = f32[4096,9]{1,0:T(8,128)S(1)} fusion(s32[2048]{0:T(1024)} %param.10, f32[2048,9]{1,0:T(8,128)S(1)} %copy.95, f32[]{:T(128)} %constant.31.clone.1), kind=kCustom, calls=%fused_computation.28 | custom fusion | flops 18432 | bytes 147968 | tf_op jit(solution)/shard_map/scatter-add | solution.py:54
  22.2 1.3 copy.96
  23.5 0.0 all-gather.4.cloned.1.call-update
  23.5 0.0 all-reduce.3.cloned.1.call-start
  24.2 0.0 copy-done.4
  24.3 0.0 copy-done
  24.3 0.0 copy-start.5
  24.3 8.6 %gather_fusion = s32[2048]{0:T(1024)S(1)} fusion(s32[1024]{0:T(1024)S(1)} %copy-done, s32[2048]{0:T(1024)S(1)} %fusion.39), kind=kCustom, calls=%fused_computation | custom fusion | bytes 24576 | tf_op jit(solution)/shard_map/jit(_take)/gather | solution.py:72
  32.9 0.0 copy-done.5
  32.9 188.1 %all-gather.4.cloned.1.call-done = f32[64,9,4096]{2,1,0:T(8,128)} async-done(((f32[1,9,4096]{2,1,0:T(8,128)}), f32[64,9,4096]{2,1,0:T(8,128)}) %all-gather.4.cloned.1.call-update) | async-done | bytes 9437200 | tf_op jit(solution)/shard_map/all_gather | solution.py:55
  221.0 6.9 reduce_sum.9
  227.9 0.0 copy-start.1
  227.9 0.0 copy-start.3
  227.9 0.2 negate_divide_fusion.2
  228.1 0.2 negate_divide_fusion.1
  228.4 0.0 copy-start.2
  228.4 0.6 copy.97
  229.1 5.5 gather_fusion.1
  234.5 0.3 copy.98
  234.9 0.0 copy-done.1
  234.9 0.0 copy-done.3
  234.9 0.1 add_convert_fusion
  235.0 0.1 slice_reduce_fusion
  235.1 0.0 copy-start.6
  235.1 1.7 fusion.4
  236.8 0.0 copy-done.2
  236.8 0.0 copy-done.6
  236.8 0.7 fusion.22
  237.6 0.7 fusion.19
  238.3 1.5 fusion.16
  239.8 0.0 all-reduce.3.cloned.1.call-update
  239.8 462.8 %all-reduce.3.cloned.1.call-done = f32[1024,128]{1,0:T(8,128)} async-done(((f32[1024,128]{1,0:T(8,128)}), f32[1024,128]{1,0:T(8,128)}) %all-reduce.3.cloned.1.call-update) | async-done | bytes 524304
  702.7 1.2 constant_dynamic-slice_fusion
  (7 shorter events, 0.1 us)
Async XLA Ops:
  7.2 17.1 %copy-start = (s32[1024]{0:T(1024)S(1)}, s32[1024]{0:T(1024)}, u32[]{:S(2)}) copy-start(s32[1024]{0:T(1024)} %param.12) | copy-start | bytes 12292
  7.2 213.8 %all-gather.4.cloned.1.call-start = ((), (), s32[]{:S(2)}) async-start(), calls=%async_computation | async-start | bytes 17039360 | tf_op jit(solution)/shard_map/all_gather | solution.py:55
  10.1 14.2 %copy-start.4 = (s32[2048]{0:T(1024)S(1)}, s32[2048]{0:T(1024)}, u32[]{:S(2)}) copy-start(s32[2048]{0:T(1024)} %param.11) | copy-start | bytes 24580
  23.5 679.1 %all-reduce.3.cloned.1.call-start = ((), (), s32[]{:S(2)}) async-start(), calls=%async_computation.1 | async-start | bytes 1048576
  24.3 8.6 %copy-start.5 = (s32[2048]{0:T(1024)S(1)}, s32[2048]{0:T(1024)}, u32[]{:S(2)}) copy-start(s32[2048]{0:T(1024)} %param.10) | copy-start | bytes 24580
  227.9 7.0 copy-start.1
  227.9 7.0 copy-start.3
  228.4 8.4 %copy-start.2 = (f32[3,4096]{1,0:T(4,128)}, f32[3,4096]{1,0:T(4,128)S(1)}, u32[]{:S(2)}) copy-start(f32[3,4096]{1,0:T(4,128)S(1)} %pad_maximum_fusion) | copy-start | bytes 147460
  235.1 1.8 copy-start.6
Sparse Core Ops, SparseCore 0:
  23.7 197.3 all-gather.3
  239.9 462.6 all-reduce.2
